TPU v7x, 32 devices: a whole 2x2x4 slice. The times are simulated.
32 devices in a mesh: grp: 2 (over y), col: 4 (over z), row: 2 (over x), limb: 2 (over core).
Axes of the slice: x: 2, y: 2, z: 4, core: 2. Of those that a mesh axis runs over, the one named last changes fastest.
Arguments:
- database: bfloat16 [8192, 8192], P(('grp', 'row'), 'col'), parts along dimension 0, may hold values from -128 to 127, as said below
- lwe_matrix: bfloat16 [8192, 2, 512], P('col', 'limb'), may hold values from -0.0008544922 to 0.0008544922
- secret_ct: float32 [2, 2, 2, 512, 4096], P(None, None, 'limb', 'col', 'row'), may hold values from -6 to 6
Outputs:
- encrypted_product: float32 [4, 2, 4096], P('grp', None, 'row'), parts along dimension 0
There are 2 independent parts, one for each index of `grp`. A program takes and returns all parts, laid end to end along the dimension named above; an argument that names none is the same for every part. Nothing has to cross between parts.
Inputs may be any that keep to these rules, and one draw needn't show every extreme that they name: `database`: whole numbers.
All inputs are finite; a program needn't handle non-finite values.
Results may differ from a plain program's by a relative error of at most 0.0003.
Values sent between devices are 32-bit elements; how exact they have to be, the bound alone decides.
A program may use at most 64 MiB of HBM per device.

v0:
```python
import math
import jax
import jax.numpy as jnp
from jax import lax
from jax.sharding import PartitionSpec as P


def exact_dot(left, right):
    return jnp.dot(left, right, precision=lax.Precision.HIGHEST, preferred_element_type=jnp.float32)


def body(database, lwe_matrix, secret_ct):
    row_count = lax.axis_size("row")
    row_rank = lax.axis_index("row")
    row_dev = database.shape[0]
    degree_all = row_dev * row_count
    sub_rows = row_dev // row_count
    a_panel = lwe_matrix[:, 0, :]
    contract_rows = (((0,), (1,)), ((), ()))
    hint_block = lax.psum_scatter(
        lax.dot_general(a_panel, database, contract_rows, preferred_element_type=jnp.float32),
        "col",
        scatter_dimension=0,
        tiled=True,
    )
    freq_low = jnp.arange(row_count, dtype=jnp.int32)
    odd_index = 2 * freq_low + 1
    by_columns = lax.all_to_all(
        hint_block[:, None, :], "row", split_axis=2, concat_axis=1, tiled=True
    )
    phase_index = freq_low[:, None] * odd_index[None, :] % (2 * row_count)
    angle_small = jnp.pi * phase_index.astype(jnp.float32) / row_count
    mixed_real = jnp.einsum(
        "jas,ak->jks", by_columns, jnp.cos(angle_small), precision=lax.Precision.HIGHEST
    )
    mixed_imag = -jnp.einsum(
        "jas,ak->jks", by_columns, jnp.sin(angle_small), precision=lax.Precision.HIGHEST
    )
    local_rows = row_rank * sub_rows + jnp.arange(sub_rows, dtype=jnp.int32)
    twist_index = odd_index[:, None] * local_rows[None, :] % (2 * degree_all)
    twist_angle = jnp.pi * twist_index.astype(jnp.float32) / degree_all
    twist_cos = jnp.cos(twist_angle)
    twist_sin = jnp.sin(twist_angle)
    turned_real = mixed_real * twist_cos + mixed_imag * twist_sin
    turned_imag = mixed_imag * twist_cos - mixed_real * twist_sin
    back_rows = lax.all_to_all(
        jnp.stack([turned_real, turned_imag]), "row", split_axis=2, concat_axis=3, tiled=True
    )
    point_real = back_rows[0, :, 0, :]
    point_imag = back_rows[1, :, 0, :]
    freq_rows = jnp.arange(row_dev, dtype=jnp.int32)
    table_index = freq_rows[:, None] * freq_rows[None, :] % row_dev
    table_angle = 2.0 * jnp.pi * table_index.astype(jnp.float32) / row_dev
    table_cos = jnp.cos(table_angle)
    table_sin = jnp.sin(table_angle)
    scale_factor = 1.0 / math.sqrt(degree_all)
    spec_real = (exact_dot(point_real, table_cos) + exact_dot(point_imag, table_sin)) * scale_factor
    spec_imag = (exact_dot(point_imag, table_cos) - exact_dot(point_real, table_sin)) * scale_factor
    cipher = secret_ct[:, :, 0]
    prod_real = jnp.sum(spec_real * cipher[:, 0] - spec_imag * cipher[:, 1], axis=1)
    prod_imag = jnp.sum(spec_real * cipher[:, 1] + spec_imag * cipher[:, 0], axis=1)
    slot_total = lax.psum(jnp.stack([prod_real, prod_imag], axis=1), ("col", "limb"))
    return slot_total / math.sqrt(2 * lwe_matrix.shape[2])


def solution(mesh):
    placed = (P(("grp", "row"), "col"), P("col", "limb", None), P(None, None, "limb", "col", "row"))
    return jax.shard_map(
        body, mesh=mesh, in_specs=placed, out_specs=P("grp", None, "row"), check_vma=False
    )
```

profile of v0, /device:TPU:0, one launch (start us, length us, event | category | flops | bytes accessed | tf_op | source)
XLA Modules:
  0.0 506.8 jit_solution(10724719638266237290)
XLA Ops:
  6.5 1.6 copy-done
  8.1 9.6 %fusion.28 = f32[512,2048]{1,0:T(8,128)} fusion(bf16[2048,2048]{1,0:T(8,128)(2,1)} %param.3, bf16[2048,1,512]{2,0,1:T(8,128)(2,1)S(1)} %copy-done), kind=kOutput, calls=%fused_computation.22 | convolution fusion | flops 4294967296 | bytes 14680064 | tf_op jit(solution)/shard_map/dot_general | solution.py:21
  17.8 79.7 %reduce-scatter.2.cloned.1.call-done = f32[128,2048]{1,0:T(8,128)} async-done(((f32[512,2048]{1,0:T(8,128)}), f32[128,2048]{1,0:T(8,128)}) %reduce-scatter.2.cloned.1.call-update) | async-done | bytes 1048592 | tf_op jit(solution)/shard_map/reduce_scatter | solution.py:20
  97.4 3.6 copy.12
  101.0 3.6 all-to-all-start
  104.6 0.2 fusion.34
  104.8 13.3 %all-to-all-done = f32[128,1,2048]{0,1,2:T(1,128)S(1)} async-done(((f32[128,1,2048]{0,1,2:T(1,128)}), f32[128,1,2048]{0,1,2:T(1,128)S(1)}, u32[]{:S(2)}, u32[]{:S(2)}) %all-to-all-start) | async-done | bytes 1048608 | tf_op jit(solution)/shard_map/all_to_all | solution.py:28
  118.1 1.0 copy-done.2
  119.1 1.6 copy.19
  120.7 3.9 convolution_negate_fusion
  124.6 4.7 add_bitcast_fusion
  129.4 0.9 pad_maximum_fusion
  130.3 0.7 copy.14
  131.0 26.6 %all_to_all.21 = f32[2,128,2,1024]{3,1,0,2:T(8,128)S(1)} all-to-all(f32[2,128,2,1024]{3,1,0,2:T(8,128)S(1)} %copy.14), channel_id=1, replica_groups=mesh['grp'=2,'col'=4,'row'=2,'limb'=2] {'row'}, dimensions={2} | all-to-all | bytes 4194304 | tf_op jit(solution)/shard_map/all_to_all | solution.py:46
  157.6 1.2 fusion.69
  158.8 2.5 copy.21
  161.3 77.7 %fusion.8 = f32[128,2048]{1,0:T(8,128)} fusion(f32[128,2048]{0,1:T(8,128)} %bitcast.52), kind=kOutput, calls=%fused_computation.11 | convolution fusion | flops 6501171200 | bytes 2097152 | tf_op jit(solution)/shard_map/dot_general | solution.py:9
  239.0 1.3 copy.20
  240.4 77.4 %fusion.10 = f32[128,2048]{1,0:T(8,128)S(1)} fusion(f32[128,2048]{0,1:T(8,128)} %bitcast.55), kind=kOutput, calls=%fused_computation.12 | convolution fusion | flops 6501171200 | bytes 2097152 | tf_op jit(solution)/shard_map/dot_general | solution.py:9
  317.8 76.7 %fusion.22 = f32[128,2048]{1,0:T(8,128)S(1)} fusion(f32[128,2048]{1,0:T(8,128)S(1)} %copy-done.5, f32[128,2048]{0,1:T(8,128)S(1)} %bitcast.56), kind=kOutput, calls=%fused_computation.17 | convolution fusion | flops 6501695488 | bytes 3145728 | tf_op jit(solution)/shard_map/dot_general | solution.py:9
  394.5 76.5 %fusion.25 = f32[128,2048]{1,0:T(8,128)S(1)} fusion(f32[128,2048]{1,0:T(8,128)S(1)} %fusion.10, f32[128,2048]{0,1:T(8,128)S(1)} %bitcast.53), kind=kOutput, calls=%fused_computation.18 | convolution fusion | flops 6501695488 | bytes 3145728 | tf_op jit(solution)/shard_map/dot_general | solution.py:9
  471.1 0.8 subtract_reduce_fusion
  471.9 27.2 %psum.7 = f32[2,2,2048]{2,0,1:T(2,128)S(1)} all-reduce(f32[2,2,2048]{2,0,1:T(2,128)S(1)} %pad_maximum_fusion.1), channel_id=1, replica_groups=mesh['grp'=2,'col'=4,'row'=2,'limb'=2] {'col','limb'}, use_global_device_ids=true, to_apply=%region_3.4 | all-reduce | flops 8192 | bytes 65536 | tf_op jit(solution)/shard_map/psum | solution.py:62
  499.1 0.6 copy.18
  (16 shorter events, 0.1 us)
Async XLA Ops:
  6.5 1.6 copy-start
  6.5 90.9 %reduce-scatter.2.cloned.1.call-start = ((), (), s32[]{:S(2)}) async-start(), calls=%async_computation.3 | async-start | bytes 5242880 | tf_op jit(solution)/shard_map/reduce_scatter | solution.py:20
  101.0 17.1 %all-to-all-start = ((f32[128,1,2048]{0,1,2:T(1,128)}), f32[128,1,2048]{0,1,2:T(1,128)S(1)}, u32[]{:S(2)}, u32[]{:S(2)}) async-start(f32[128,1,2048]{0,1,2:T(1,128)} %copy.12), calls=%async_computation.1 | async-start | bytes 2097152 | tf_op jit(solution)/shard_map/all_to_all | solution.py:28
  118.1 1.0 copy-start.2
  240.4 77.4 %copy-start.4 = (f32[1,128,2,1024]{1,3,2,0:T(8,128)S(1)}, f32[1,128,2,1024]{1,3,2,0:T(8,128)}, u32[]{:S(2)}) copy-start(f32[1,128,2,1024]{1,3,2,0:T(8,128)} %copy.20) | copy-start | bytes 3145732
  240.4 77.4 %copy-start.5 = (f32[128,2048]{1,0:T(8,128)S(1)}, f32[128,2048]{1,0:T(8,128)}, u32[]{:S(2)}) copy-start(f32[128,2048]{1,0:T(8,128)} %fusion.8) | copy-start | bytes 3145732
  317.8 76.8 %copy-start.3 = (f32[1,128,2,1024]{1,3,2,0:T(8,128)S(1)}, f32[1,128,2,1024]{1,3,2,0:T(8,128)}, u32[]{:S(2)}) copy-start(f32[1,128,2,1024]{1,3,2,0:T(8,128)} %copy.21) | copy-start | bytes 3145732
  394.5 76.5 %copy-start.1 = (f32[2,2,1,128,2048]{4,3,2,1,0:T(8,128)S(1)}, f32[2,2,1,128,2048]{4,3,2,1,0:T(8,128)}, u32[]{:S(2)}) copy-start(f32[2,2,1,128,2048]{4,3,2,1,0:T(8,128)} %param.5) | copy-start | bytes 12582916
Sparse Core Ops, SparseCore 0:
  17.9 79.5 reduce-scatter.1
where the time goes:
time: 514 us; the launch traced here: 507 us
  matrix products  327 us (64%)
  waiting for transfers between devices  93 us (18%)
  blocking collectives  53.8 us (10%)
  local copies, waits for them, and re-layouts  14.1 us (3%)
  between operations  13.7 us (3%)
    dot_general x4, matrix products, exact_dot(): jnp.dot(left, right, precision=lax.Precision.HIGHEST, preferred_element_t...  308 us
    reduce_scatter x1, waiting for transfers between devices, body(): lax.psum_scatter(lax.dot_general(a_panel, database, contract_rows, prefer...  79.7 us
    psum x1, blocking collectives, body(): lax.psum(jnp.stack([prod_real, prod_imag], axis=1), ('col', 'limb'))  27.2 us
    all_to_all x1, blocking collectives, body(): lax.all_to_all(jnp.stack([turned_real, turned_imag]), 'row', split_axis=2...  26.6 us
    all_to_all x1, waiting for transfers between devices, body(): lax.all_to_all(hint_block[:, None, :], 'row', split_axis=2, concat_axis=1...  13.3 us
  transfers between devices with their start and end apart: 2, of which 2 were waited for; matrix products, arithmetic and copies ran while one was open for 0% of the time, Pallas kernels for 0%

commit v1 on v0

--- a/solution.py
+++ b/solution.py
@@ -59,7 +59,9 @@
     cipher = secret_ct[:, :, 0]
     prod_real = jnp.sum(spec_real * cipher[:, 0] - spec_imag * cipher[:, 1], axis=1)
     prod_imag = jnp.sum(spec_real * cipher[:, 1] + spec_imag * cipher[:, 0], axis=1)
-    slot_total = lax.psum(jnp.stack([prod_real, prod_imag], axis=1), ("col", "limb"))
+    part = jnp.stack([prod_real, prod_imag], axis=1)
+    blocks = lax.all_gather(part, ("col", "limb"), axis=0, tiled=False)
+    slot_total = blocks.sum(axis=0)
     return slot_total / math.sqrt(2 * lwe_matrix.shape[2])
 
 

time: 514 us -> 502 us (0.977)
  blocking collectives: 53.8 us -> 42 us
    psum x1 -> x0, blocking collectives: 27.2 us -> none  [body(): lax.psum(jnp.stack([prod_real, prod_imag], axis=1), ('col', 'limb'))]
    all_gather x0 -> x1, blocking collectives: none -> 15.3 us  [body(): blocks = lax.all_gather(part, ('col', 'limb'), axis=0, tiled=False)]
where the time goes in v1:
time: 502 us; the launch traced here: 495 us
  matrix products  327 us (65%)
  waiting for transfers between devices  93 us (19%)
  blocking collectives  42 us (8%)
  between operations  13.8 us (3%)
  local copies, waits for them, and re-layouts  13.5 us (3%)
    dot_general x4, matrix products, exact_dot(): jnp.dot(left, right, precision=lax.Precision.HIGHEST, preferred_element_t...  308 us
    reduce_scatter x1, waiting for transfers between devices, body(): lax.psum_scatter(lax.dot_general(a_panel, database, contract_rows, prefer...  79.7 us
    all_to_all x1, blocking collectives, body(): lax.all_to_all(jnp.stack([turned_real, turned_imag]), 'row', split_axis=2...  26.6 us
    all_gather x1, blocking collectives, body(): blocks = lax.all_gather(part, ('col', 'limb'), axis=0, tiled=False)  15.3 us
    all_to_all x1, waiting for transfers between devices, body(): lax.all_to_all(hint_block[:, None, :], 'row', split_axis=2, concat_axis=1...  13.3 us
  transfers between devices with their start and end apart: 2, of which 2 were waited for; matrix products, arithmetic and copies ran while one was open for 0% of the time, Pallas kernels for 0%

profile of v1, /device:TPU:0, one launch (start us, length us, event | category | flops | bytes accessed | tf_op | source)
XLA Modules:
  0.0 495.1 jit_solution(14232134233034930929)
XLA Ops:
  6.5 1.6 copy-done
  8.1 9.6 %fusion.28 = f32[512,2048]{1,0:T(8,128)} fusion(bf16[2048,2048]{1,0:T(8,128)(2,1)} %param.3, bf16[2048,1,512]{2,0,1:T(8,128)(2,1)S(1)} %copy-done), kind=kOutput, calls=%fused_computation.22 | convolution fusion | flops 4294967296 | bytes 14680064 | tf_op jit(solution)/shard_map/dot_general | solution.py:21
  17.8 79.7 %reduce-scatter.2.cloned.1.call-done = f32[128,2048]{1,0:T(8,128)} async-done(((f32[512,2048]{1,0:T(8,128)}), f32[128,2048]{1,0:T(8,128)}) %reduce-scatter.2.cloned.1.call-update) | async-done | bytes 1048592 | tf_op jit(solution)/shard_map/reduce_scatter | solution.py:20
  97.4 3.6 copy.9
  101.0 3.6 all-to-all-start
  104.6 0.2 fusion.34
  104.8 13.3 %all-to-all-done = f32[128,1,2048]{0,1,2:T(1,128)S(1)} async-done(((f32[128,1,2048]{0,1,2:T(1,128)}), f32[128,1,2048]{0,1,2:T(1,128)S(1)}, u32[]{:S(2)}, u32[]{:S(2)}) %all-to-all-start) | async-done | bytes 1048608 | tf_op jit(solution)/shard_map/all_to_all | solution.py:28
  118.1 1.0 copy-done.2
  119.1 1.6 copy.15
  120.7 3.9 convolution_negate_fusion
  124.6 4.7 add_bitcast_fusion
  129.4 0.9 pad_maximum_fusion
  130.3 0.7 copy.11
  131.0 26.6 %all_to_all.21 = f32[2,128,2,1024]{3,1,0,2:T(8,128)S(1)} all-to-all(f32[2,128,2,1024]{3,1,0,2:T(8,128)S(1)} %copy.11), channel_id=1, replica_groups=mesh['grp'=2,'col'=4,'row'=2,'limb'=2] {'row'}, dimensions={2} | all-to-all | bytes 4194304 | tf_op jit(solution)/shard_map/all_to_all | solution.py:46
  157.6 1.2 fusion.69
  158.8 2.5 copy.17
  161.3 77.7 %fusion.8 = f32[128,2048]{1,0:T(8,128)} fusion(f32[128,2048]{0,1:T(8,128)} %bitcast.52), kind=kOutput, calls=%fused_computation.11 | convolution fusion | flops 6501171200 | bytes 2097152 | tf_op jit(solution)/shard_map/dot_general | solution.py:9
  239.0 1.3 copy.16
  240.4 77.4 %fusion.10 = f32[128,2048]{1,0:T(8,128)S(1)} fusion(f32[128,2048]{0,1:T(8,128)} %bitcast.55), kind=kOutput, calls=%fused_computation.12 | convolution fusion | flops 6501171200 | bytes 2097152 | tf_op jit(solution)/shard_map/dot_general | solution.py:9
  317.8 76.7 %fusion.22 = f32[128,2048]{1,0:T(8,128)S(1)} fusion(f32[128,2048]{1,0:T(8,128)S(1)} %copy-done.5, f32[128,2048]{0,1:T(8,128)S(1)} %bitcast.56), kind=kOutput, calls=%fused_computation.17 | convolution fusion | flops 6501695488 | bytes 3145728 | tf_op jit(solution)/shard_map/dot_general | solution.py:9
  394.5 76.5 %fusion.25 = f32[128,2048]{1,0:T(8,128)S(1)} fusion(f32[128,2048]{1,0:T(8,128)S(1)} %fusion.10, f32[128,2048]{0,1:T(8,128)S(1)} %bitcast.53), kind=kOutput, calls=%fused_computation.18 | convolution fusion | flops 6501695488 | bytes 3145728 | tf_op jit(solution)/shard_map/dot_general | solution.py:9
  471.1 0.8 subtract_reduce_fusion
  472.0 15.3 %all-gather = f32[16,2,2048]{2,1,0:T(2,128)S(1)} all-gather(f32[2,2,2048]{2,1,0:T(2,128)S(1)} %pad_maximum_fusion.1), channel_id=2, replica_groups=mesh['grp'=2,'col'=4,'row'=2,'limb'=2] {'col','limb'}, dimensions={0}, use_global_device_ids=true | all-gather | bytes 294912 | tf_op jit(solution)/shard_map/all_gather | solution.py:63
  487.4 0.6 broadcast_multiply_fusion
  (18 shorter events, 0.2 us)
Async XLA Ops:
  6.5 1.6 copy-start
  6.5 90.9 %reduce-scatter.2.cloned.1.call-start = ((), (), s32[]{:S(2)}) async-start(), calls=%async_computation.3 | async-start | bytes 5242880 | tf_op jit(solution)/shard_map/reduce_scatter | solution.py:20
  101.0 17.1 %all-to-all-start = ((f32[128,1,2048]{0,1,2:T(1,128)}), f32[128,1,2048]{0,1,2:T(1,128)S(1)}, u32[]{:S(2)}, u32[]{:S(2)}) async-start(f32[128,1,2048]{0,1,2:T(1,128)} %copy.9), calls=%async_computation.1 | async-start | bytes 2097152 | tf_op jit(solution)/shard_map/all_to_all | solution.py:28
  118.1 1.0 copy-start.2
  240.4 77.4 %copy-start.4 = (f32[1,128,2,1024]{1,3,2,0:T(8,128)S(1)}, f32[1,128,2,1024]{1,3,2,0:T(8,128)}, u32[]{:S(2)}) copy-start(f32[1,128,2,1024]{1,3,2,0:T(8,128)} %copy.16) | copy-start | bytes 3145732
  240.4 77.4 %copy-start.5 = (f32[128,2048]{1,0:T(8,128)S(1)}, f32[128,2048]{1,0:T(8,128)}, u32[]{:S(2)}) copy-start(f32[128,2048]{1,0:T(8,128)} %fusion.8) | copy-start | bytes 3145732
  317.8 76.8 %copy-start.3 = (f32[1,128,2,1024]{1,3,2,0:T(8,128)S(1)}, f32[1,128,2,1024]{1,3,2,0:T(8,128)}, u32[]{:S(2)}) copy-start(f32[1,128,2,1024]{1,3,2,0:T(8,128)} %copy.17) | copy-start | bytes 3145732
  394.5 76.5 %copy-start.1 = (f32[2,2,1,128,2048]{4,3,2,1,0:T(8,128)S(1)}, f32[2,2,1,128,2048]{4,3,2,1,0:T(8,128)}, u32[]{:S(2)}) copy-start(f32[2,2,1,128,2048]{4,3,2,1,0:T(8,128)} %param.5) | copy-start | bytes 12582916
Sparse Core Ops, SparseCore 0:
  17.9 79.5 reduce-scatter.1
